TPU v7x, 128 devices: a whole 4x4x4 slice. The times are simulated.
128 devices in a mesh: row: 4 (over x), col: 32 (over y, z, core).
Axes of the slice: x: 4, y: 4, z: 4, core: 2. Of those that a mesh axis runs over, the one named last changes fastest.
Arguments:
- ancestor_inverse: float32 [16384, 16384], P('col', 'row'), as said below
- panels: float32 [2, 16384, 512], P(None, ('col', 'row')), may hold values from -0.1875 to 0.1875
- pattern: int32 [2, 128, 2], replicated, may hold values 0 or 1
- diag_inverse: float32 [2, 512, 512], replicated, may hold values from -6 to 6
- link_panel: float32 [512, 512], replicated, may hold values from -0.25 to 0.25
- block_list: int32 [32, 4, 32], P('col', 'row'), may hold values from 0 to 7
- gauge_owner: int32 [32, 4, 32], P('col', 'row'), may hold values from 0 to 31, each once within a row
- gauge_weight: float32 [4, 32, 512], P('row', 'col'), may hold values from -0.25 to 0.25
Outputs:
- y_first: float32 [16384, 512], P(('col', 'row'))
- diag_first: float32 [512, 512], replicated
- y_second: float32 [16384, 512], P(('col', 'row'))
- cross_second: float32 [512, 512], replicated
- diag_second: float32 [512, 512], replicated
- gauge_response: float32 [4, 32, 512], P('row', 'col')
Inputs may be any that keep to these rules, and one draw needn't show every extreme that they name: `ancestor_inverse`: with its columns put in natural order the matrix is symmetric.
All inputs are finite; a program needn't handle non-finite values.
Results may differ from a plain program's by a relative error of at most 0.000092.
Values sent between devices are 32-bit elements; how exact they have to be, the bound alone decides.
No kernel may reach another device: no remote copies, remote signals or barrier semaphores. Data moves between devices by JAX's collectives and lax.ppermute only.
A program may use at most 128 MiB of HBM per device.

v0:
```python
import jax
import jax.numpy as jnp
from jax import lax
from jax.sharding import PartitionSpec as P

NIB = 8
HIGHEST_PRECISION = lax.Precision.HIGHEST


def matmul(left, right):
    return jnp.dot(left, right, precision=HIGHEST_PRECISION, preferred_element_type=jnp.float32)


def inner_product(left, right):
    return lax.dot_general(
        left,
        right,
        (((0,), (0,)), ((), ())),
        precision=HIGHEST_PRECISION,
        preferred_element_type=jnp.float32,
    )


def apply_pattern(panel, pattern_step, seg_index):
    tile_flags = lax.dynamic_index_in_dim(pattern_step, seg_index, 0, keepdims=False).astype(
        jnp.float32
    )
    seg_rows, panel_width = panel.shape
    tile_count = tile_flags.shape[0]
    shaped = (
        panel.reshape(seg_rows, tile_count, panel_width // tile_count) * tile_flags[None, :, None]
    )
    return shaped.reshape(seg_rows, panel_width)


def inverse_slab(ancestor, panel_seg):
    partial_rows = matmul(ancestor, lax.all_gather(panel_seg, "col", axis=0, tiled=True))
    return lax.psum_scatter(partial_rows, "row", scatter_dimension=0, tiled=True)


def local(
    ancestor_inverse,
    panels,
    pattern,
    diag_inverse,
    link_panel,
    block_list,
    gauge_owner,
    gauge_weight,
):
    grid_rows = lax.axis_size("row")
    grid_cols = lax.axis_size("col")
    seg_index = lax.axis_index("col") * grid_rows + lax.axis_index("row")
    first_panel = apply_pattern(panels[0], pattern[0], seg_index)
    second_panel = apply_pattern(panels[1], pattern[1], seg_index)
    y_first = -inverse_slab(ancestor_inverse, first_panel)
    first_terms = lax.psum(inner_product(first_panel, y_first), ("row", "col"))
    diag_first = diag_inverse[0] - first_terms
    cross_terms = lax.psum(inner_product(y_first, second_panel), ("row", "col"))
    y_second = -(inverse_slab(ancestor_inverse, second_panel) + matmul(y_first, link_panel))
    second_terms = lax.psum(inner_product(second_panel, y_second), ("row", "col"))
    cross_second = -(cross_terms + matmul(diag_first, link_panel))
    diag_second = diag_inverse[1] - second_terms - inner_product(link_panel, cross_second)
    seg_rows, panel_width = y_second.shape
    block_rows = seg_rows // NIB
    blocks = y_second.reshape(NIB, block_rows * panel_width)
    owners = gauge_owner[0, 0]
    picks = block_list[0, 0]
    owner_match = (owners[None, :] == jnp.arange(grid_cols, dtype=jnp.int32)[:, None]).astype(
        jnp.float32
    )
    block_match = (picks[:, None] == jnp.arange(NIB, dtype=jnp.int32)[None, :]).astype(jnp.float32)
    selector = matmul(owner_match, block_match)
    outgoing = matmul(selector, blocks)
    received = lax.all_to_all(outgoing, "col", split_axis=0, concat_axis=0, tiled=True)
    received_rows = received.reshape(grid_cols * block_rows, panel_width)
    weights = gauge_weight[0, 0]
    gauge_response = matmul(weights[None, :], received_rows).reshape(1, 1, panel_width)
    return (y_first, diag_first, y_second, cross_second, diag_second, gauge_response)


def solution(mesh):
    in_specs = (
        P("col", "row"),
        P(None, ("col", "row"), None),
        P(),
        P(),
        P(),
        P("col", "row", None),
        P("col", "row", None),
        P("row", "col", None),
    )
    out_specs = (
        P(("col", "row"), None),
        P(),
        P(("col", "row"), None),
        P(),
        P(),
        P("row", "col", None),
    )
    return jax.shard_map(local, mesh=mesh, in_specs=in_specs, out_specs=out_specs, check_vma=False)
```

profile of v0, /device:TPU:1, one launch (start us, length us, event | category | flops | bytes accessed | tf_op | source)
XLA Modules:
  0.0 363.5 jit_solution(13496992720899328515)
XLA Ops:
  7.2 0.0 copy-start
  7.2 0.0 all-gather.3.cloned.1.call-start
  7.2 0.8 fusion.12
  8.0 0.2 convert_reduce_fusion
  8.2 0.1 broadcast_bitcast_fusion.1
  8.3 0.1 broadcast_bitcast_fusion
  8.4 1.9 bitcast_multiply_fusion
  10.3 0.0 all-gather.3.cloned.1.call-update
  10.3 0.0 all-gather.5.cloned.1.call-start
  10.3 0.7 all-gather.5.cloned.1.call-update
  11.0 0.0 reduce-scatter.3.cloned.1.call-start
  11.1 56.5 %all-gather.3.cloned.1.call-done = f32[4096,512]{1,0:T(8,128)} async-done(((f32[128,512]{1,0:T(8,128)}), f32[4096,512]{1,0:T(8,128)}) %all-gather.3.cloned.1.call-update) | async-done | bytes 8388624 | tf_op jit(solution)/shard_map/all_gather | solution.py:37
  67.5 30.1 %convolution_bitcast_fusion.3 = f32[512,512]{0,1:T(8,128)} fusion(f32[4096,512]{1,0:T(8,128)} %all-gather.3.cloned.1.call-done, f32[512,4096]{1,0:T(8,128)} %param.8), kind=kOutput, calls=%fused_computation.6 | convolution fusion | flops 12884901888 | bytes 17825792 | tf_op jit(solution)/shard_map/dot_general | solution.py:11
  97.6 0.0 reduce-scatter.3.cloned.1.call-update
  97.6 0.0 copy-start.4
  97.6 0.0 copy-start.5
  97.7 0.2 reduce-scatter.5.cloned.1.call-start
  97.9 25.0 %all-gather.5.cloned.1.call-done = f32[4096,512]{1,0:T(8,128)} async-done(((f32[128,512]{1,0:T(8,128)}), f32[4096,512]{1,0:T(8,128)}) %all-gather.5.cloned.1.call-update) | async-done | bytes 8388624 | tf_op jit(solution)/shard_map/all_gather | solution.py:37
  122.9 30.1 %convolution_bitcast_fusion.2 = f32[512,512]{0,1:T(8,128)} fusion(f32[4096,512]{1,0:T(8,128)} %all-gather.5.cloned.1.call-done, f32[512,4096]{1,0:T(8,128)} %param.8), kind=kOutput, calls=%fused_computation.5 | convolution fusion | flops 12884901888 | bytes 17825792 | tf_op jit(solution)/shard_map/dot_general | solution.py:11
  153.0 0.0 copy-start.8
  153.0 0.0 copy-start.9
  153.0 0.0 reduce-scatter.5.cloned.1.call-update
  153.0 0.3 all-reduce.3.cloned.1.call-start
  153.3 0.0 reduce-scatter.3.cloned.1.call-done
  153.3 0.0 copy-start.3
  153.3 21.1 %reduce-scatter.5.cloned.1.call-done = f32[128,512]{0,1:T(8,128)} async-done(((f32[512,512]{0,1:T(8,128)}), f32[128,512]{0,1:T(8,128)}) %reduce-scatter.5.cloned.1.call-update) | async-done | bytes 262160 | tf_op jit(solution)/shard_map/reduce_scatter | solution.py:38
  174.4 0.0 copy-done
  174.4 2.8 fusion.2
  177.3 0.0 copy-done.4
  177.3 2.0 fusion.13
  179.3 2.9 fusion.7
  182.2 0.0 copy-done.5
  182.2 0.0 copy-start.7
  182.2 3.0 fusion.10
  185.1 0.0 all-reduce.3.cloned.1.call-update
  185.2 0.0 copy-done.8
  185.2 0.0 copy-done.9
  185.2 0.2 fusion.3
  185.4 0.1 copy.28
  185.6 0.0 copy-start.6
  185.6 0.1 reshape.54
  185.6 1.0 convolution_bitcast_fusion
  186.7 2.1 copy.26
  188.7 0.0 copy-done.6
  188.7 9.0 %all-to-all-start = ((f32[32,1,8192]{2,1,0:T(1,128)}), f32[32,1,8192]{2,1,0:T(1,128)S(1)}, u32[]{:S(2)}, u32[]{:S(2)}) async-start(f32[32,1,8192]{2,1,0:T(1,128)} %copy.26), calls=%async_computation.2 | async-start | bytes 2097152 | tf_op jit(solution)/shard_map/all_to_all | solution.py:75
  197.8 0.0 copy-done.3
  197.8 0.8 copy.27
  198.6 17.2 %all-to-all-done = f32[32,1,8192]{2,1,0:T(1,128)S(1)} async-done(((f32[32,1,8192]{2,1,0:T(1,128)}), f32[32,1,8192]{2,1,0:T(1,128)S(1)}, u32[]{:S(2)}, u32[]{:S(2)}) %all-to-all-start) | async-done | bytes 1048608 | tf_op jit(solution)/shard_map/all_to_all | solution.py:75
  215.9 2.6 reduce.2
  218.5 0.2 reshape.55
  218.7 0.0 copy-done.7
  218.7 1.2 convolution_bitcast_fusion.4
  219.9 127.0 %all-reduce.3.cloned.1.call-done = (f32[512,512]{1,0:T(8,128)}, f32[512,512]{1,0:T(8,128)}, f32[512,512]{1,0:T(8,128)}) async-done(((f32[512,512]{1,0:T(8,128)}, f32[512,512]{1,0:T(8,128)}, f32[512,512]{1,0:T(8,128)}), (f32[512,512]{1,0:T(8,128)}, f32[512,512]{1,0:T(8,128)}, f32[512,512]{1,0:T(8,128)})) %all-reduce.3.cloned.1.call-update) | async-done | bytes 3145744 | tf_op jit(solution)/shard_map/psum | solution.py:57
  346.9 1.7 bitcast_subtract_fusion.1
  348.6 0.0 copy-start.1
  348.6 3.5 fusion.1
  352.2 0.0 copy-start.2
  352.2 4.8 %fusion = f32[512,512]{1,0:T(8,128)} fusion(f32[512,512]{1,0:T(8,128)S(1)} %fusion.1, f32[512,512]{1,0:T(8,128)S(1)} %copy-done, f32[512,512]{1,0:T(8,128)} %get-tuple-element.26, f32[2,512,512]{2,1,0:T(8,128)} %param.11), kind=kOutput, calls=%fused_computation.2 | convolution fusion | flops 1611137024 | bytes 5242880 | tf_op jit(solution)/shard_map/dot_general | solution.py:15
  356.9 0.0 copy-done.1
  356.9 0.0 copy-done.2
  (3 shorter events, 0.0 us)
Async XLA Ops:
  7.2 167.3 %copy-start = (f32[512,512]{1,0:T(8,128)S(1)}, f32[512,512]{1,0:T(8,128)}, u32[]{:S(2)}) copy-start(f32[512,512]{1,0:T(8,128)} %param.12) | copy-start | bytes 3145732
  7.2 60.4 %all-gather.3.cloned.1.call-start = ((), (), s32[]{:S(2)}) async-start(), calls=%async_computation.3 | async-start | bytes 8650752 | tf_op jit(solution)/shard_map/all_gather | solution.py:37
  10.3 112.6 %all-gather.5.cloned.1.call-start = ((), (), s32[]{:S(2)}) async-start(), calls=%async_computation.5 | async-start | bytes 8650752 | tf_op jit(solution)/shard_map/all_gather | solution.py:37
  11.0 142.3 %reduce-scatter.3.cloned.1.call-start = ((), (), s32[]{:S(2)}) async-start(), calls=%async_computation.4 | async-start | bytes 1310720 | tf_op jit(solution)/shard_map/reduce_scatter | solution.py:38
  97.6 79.6 %copy-start.4 = (f32[128,512]{1,0:T(8,128)S(1)}, f32[128,512]{1,0:T(8,128)}, u32[]{:S(2)}) copy-start(f32[128,512]{1,0:T(8,128)} %get-tuple-element.27) | copy-start | bytes 786436
  97.6 84.5 %copy-start.5 = (f32[128,512]{1,0:T(8,128)S(1)}, f32[128,512]{1,0:T(8,128)}, u32[]{:S(2)}) copy-start(f32[128,512]{1,0:T(8,128)} %get-tuple-element.28) | copy-start | bytes 786436
  97.7 76.8 %reduce-scatter.5.cloned.1.call-start = ((), (), s32[]{:S(2)}) async-start(), calls=%async_computation.6 | async-start | bytes 1310720 | tf_op jit(solution)/shard_map/reduce_scatter | solution.py:38
  153.0 32.2 %copy-start.8 = (s32[1,1,32]{2,1,0:T(1,128)S(1)}, s32[1,1,32]{2,1,0:T(1,128)}, u32[]{:S(2)}) copy-start(s32[1,1,32]{2,1,0:T(1,128)} %param.13) | copy-start | bytes 388
  153.0 32.2 %copy-start.9 = (s32[1,1,32]{2,1,0:T(1,128)S(1)}, s32[1,1,32]{2,1,0:T(1,128)}, u32[]{:S(2)}) copy-start(s32[1,1,32]{2,1,0:T(1,128)} %param.14) | copy-start | bytes 388
  153.0 193.8 %all-reduce.3.cloned.1.call-start = ((), (), s32[]{:S(2)}) async-start(), calls=%async_computation.7 | async-start | bytes 6291456 | tf_op jit(solution)/shard_map/psum | solution.py:57
  153.3 44.4 %copy-start.3 = (f32[128,512]{0,1:T(8,128)S(1)}, f32[128,512]{0,1:T(8,128)}, u32[]{:S(2)}) copy-start(f32[128,512]{0,1:T(8,128)} %reduce-scatter.3.cloned.1.call-done) | copy-start | bytes 786436
  182.2 36.5 %copy-start.7 = (f32[1,1,512]{2,1,0:T(1,128)S(1)}, f32[1,1,512]{2,1,0:T(1,128)}, u32[]{:S(2)}) copy-start(f32[1,1,512]{2,1,0:T(1,128)} %param.15) | copy-start | bytes 6148
  185.6 3.2 copy-start.6
  188.7 27.2 %all-to-all-start = ((f32[32,1,8192]{2,1,0:T(1,128)}), f32[32,1,8192]{2,1,0:T(1,128)S(1)}, u32[]{:S(2)}, u32[]{:S(2)}) async-start(f32[32,1,8192]{2,1,0:T(1,128)} %copy.26), calls=%async_computation.2 | async-start | bytes 2097152 | tf_op jit(solution)/shard_map/all_to_all | solution.py:75
  348.6 8.3 %copy-start.1 = (f32[512,512]{1,0:T(8,128)}, f32[512,512]{1,0:T(8,128)S(1)}, u32[]{:S(2)}) copy-start(f32[512,512]{1,0:T(8,128)S(1)} %bitcast_subtract_fusion.1) | copy-start | bytes 3145732
  352.2 4.8 %copy-start.2 = (f32[512,512]{1,0:T(8,128)}, f32[512,512]{1,0:T(8,128)S(1)}, u32[]{:S(2)}) copy-start(f32[512,512]{1,0:T(8,128)S(1)} %fusion.1) | copy-start | bytes 3145732
Sparse Core Ops, SparseCore 0:
  10.9 56.6 all-gather.2
  70.4 52.5 all-gather.4
  125.9 21.1 reduce-scatter.2
  153.2 21.2 reduce-scatter.4
  185.3 161.5 all-reduce.2
where the time goes:
time: 364 us; the launch traced here: 363 us
  waiting for transfers between devices  248 us (68%)
  matrix products  81.6 us (22%)
  between operations  14 us (4%)
  starting transfers between devices  9.63 us (3%)
  other arithmetic  6.45 us (2%)
  local copies, waits for them, and re-layouts  4.26 us (1%)
    psum x1, waiting for transfers between devices, local(): first_terms = lax.psum(inner_product(first_panel, y_first), ('row', 'col'))  127 us
    all_gather x2, waiting for transfers between devices, inverse_slab(): lax.all_gather(panel_seg, 'col', axis=0, tiled=True)  81.5 us
    dot_general x7, matrix products, matmul(): jnp.dot(left, right, precision=HIGHEST_PRECISION, preferred_element_type=...  69 us
    reduce_scatter x2, waiting for transfers between devices, inverse_slab(): lax.psum_scatter(partial_rows, 'row', scatter_dimension=0, tiled=True)  21.1 us
    all_to_all x1, waiting for transfers between devices, local(): lax.all_to_all(outgoing, 'col', split_axis=0, concat_axis=0, tiled=True)  17.2 us
    dot_general x4, matrix products, inner_product(): lax.dot_general(left, right, (((0,), (0,)), ((), ())), precision=HIGHEST_...  12.6 us
    all_to_all x1, starting transfers between devices, local(): lax.all_to_all(outgoing, 'col', split_axis=0, concat_axis=0, tiled=True)  9.03 us
  transfers between devices with their start and end apart: 6, of which 5 were waited for; matrix products, arithmetic and copies ran while one was open for 19% of the time, Pallas kernels for 0%

commit v1 on v0

--- a/solution.py
+++ b/solution.py
@@ -5,6 +5,13 @@
 
 NIB = 8
 HIGHEST_PRECISION = lax.Precision.HIGHEST
+
+
+def _answer_plate(q_in, peer_axis, pos_dim=0):
+    seen_now = lax.axis_size(peer_axis)
+    mat_out = jnp.stack([q_in] * seen_now, 0)
+    s_next = lax.all_to_all(mat_out, peer_axis, 0, 0)
+    return jnp.concatenate(s_next, pos_dim)
 
 
 def matmul(left, right):
@@ -34,7 +41,7 @@
 
 
 def inverse_slab(ancestor, panel_seg):
-    partial_rows = matmul(ancestor, lax.all_gather(panel_seg, "col", axis=0, tiled=True))
+    partial_rows = matmul(ancestor, _answer_plate(panel_seg, "col"))
     return lax.psum_scatter(partial_rows, "row", scatter_dimension=0, tiled=True)
 
 

time: 364 us -> 491 us (1.35)
  blocking collectives: 0 us -> 105 us
  waiting for transfers between devices: 248 us -> 260 us
  local copies, waits for them, and re-layouts: 4.26 us -> 9.64 us
    all_to_all x0 -> x1, blocking collectives: none -> 105 us  [_answer_plate(): s_next = lax.all_to_all(mat_out, peer_axis, 0, 0)]
    all_gather x2 -> x0, waiting for transfers between devices: 81.5 us -> none  [inverse_slab(): lax.all_gather(panel_seg, 'col', axis=0, tiled=True)]
    all_to_all x0 -> x1, waiting for transfers between devices: none -> 76.3 us  [_answer_plate(): s_next = lax.all_to_all(mat_out, peer_axis, 0, 0)]
    reduce_scatter x2, waiting for transfers between devices: 21.1 us -> 39.1 us  [inverse_slab(): lax.psum_scatter(partial_rows, 'row', scatter_dimension=0, tiled=True)]
    another operation x0 -> x2, local copies, waits for them, and re-layouts: none -> 5.37 us  [_answer_plate(): mat_out = jnp.stack([q_in] * seen_now, 0)]
  transfers between devices with their start and end apart: 6 -> 5, of which waited for: 5 -> 4; matrix products, arithmetic and copies ran while one was open for 19% -> 14% of each run, Pallas kernels for 0% -> 0%
where the time goes in v1:
time: 491 us; the launch traced here: 490 us
  waiting for transfers between devices  260 us (53%)
  blocking collectives  105 us (21%)
  matrix products  81.7 us (17%)
  starting transfers between devices  14.4 us (3%)
  between operations  13.9 us (3%)
  local copies, waits for them, and re-layouts  9.64 us (2%)
  other arithmetic  5.65 us (1%)
    psum x1, waiting for transfers between devices, local(): first_terms = lax.psum(inner_product(first_panel, y_first), ('row', 'col'))  127 us
    all_to_all x1, blocking collectives, _answer_plate(): s_next = lax.all_to_all(mat_out, peer_axis, 0, 0)  105 us
    all_to_all x1, waiting for transfers between devices, _answer_plate(): s_next = lax.all_to_all(mat_out, peer_axis, 0, 0)  76.3 us
    dot_general x7, matrix products, matmul(): jnp.dot(left, right, precision=HIGHEST_PRECISION, preferred_element_type=...  69 us
    reduce_scatter x2, waiting for transfers between devices, inverse_slab(): lax.psum_scatter(partial_rows, 'row', scatter_dimension=0, tiled=True)  39.1 us
    all_to_all x1, waiting for transfers between devices, local(): lax.all_to_all(outgoing, 'col', split_axis=0, concat_axis=0, tiled=True)  17.3 us
    dot_general x4, matrix products, inner_product(): lax.dot_general(left, right, (((0,), (0,)), ((), ())), precision=HIGHEST_...  12.7 us
  transfers between devices with their start and end apart: 5, of which 4 were waited for; matrix products, arithmetic and copies ran while one was open for 14% of the time, Pallas kernels for 0%

profile of v1, /device:TPU:1, one launch (start us, length us, event | category | flops | bytes accessed | tf_op | source)
XLA Modules:
  0.0 490.0 jit_solution(15511132333516795812)
XLA Ops:
  7.2 0.0 copy-start
  7.2 0.8 fusion.19
  8.0 0.2 convert_reduce_fusion
  8.2 0.1 broadcast_bitcast_fusion
  8.3 0.1 broadcast_bitcast_fusion.1
  8.3 1.1 multiply_bitcast_fusion
  9.4 1.1 stack.6
  10.5 105.1 %all_to_all.19 = f32[32,128,512]{2,1,0:T(8,128)} all-to-all(f32[32,128,512]{2,1,0:T(8,128)S(1)} %stack.6), channel_id=1, replica_groups=mesh['row'=4,'col'=32] {'col'}, dimensions={0} | all-to-all | bytes 16777216 | tf_op jit(solution)/shard_map/all_to_all | solution.py:13
  115.6 4.3 stack.7
  119.9 4.8 all-to-all-start.1
  124.6 0.0 reduce-scatter.3.cloned.1.call-start
  124.7 30.1 %convolution_bitcast_fusion.3 = f32[512,512]{0,1:T(8,128)} fusion(f32[4096,512]{1,0:T(8,128)} %bitcast.59, f32[512,4096]{1,0:T(8,128)} %param.8), kind=kOutput, calls=%fused_computation.6 | convolution fusion | flops 12884901888 | bytes 17825792 | tf_op jit(solution)/shard_map/dot_general | solution.py:18
  154.8 0.0 reduce-scatter.3.cloned.1.call-update
  154.8 0.2 reduce-scatter.5.cloned.1.call-start
  155.0 76.3 %all-to-all-done.1 = f32[32,128,512]{2,1,0:T(8,128)} async-done(((f32[32,128,512]{2,1,0:T(8,128)}), f32[32,128,512]{2,1,0:T(8,128)}, u32[]{:S(2)}, u32[]{:S(2)}) %all-to-all-start.1) | async-done | bytes 8388640 | tf_op jit(solution)/shard_map/all_to_all | solution.py:13
  231.4 0.0 copy-start.4
  231.4 30.1 %convolution_bitcast_fusion.2 = f32[512,512]{0,1:T(8,128)} fusion(f32[4096,512]{1,0:T(8,128)} %bitcast.6, f32[512,4096]{1,0:T(8,128)} %param.8), kind=kOutput, calls=%fused_computation.5 | convolution fusion | flops 12884901888 | bytes 17825792 | tf_op jit(solution)/shard_map/dot_general | solution.py:18
  261.5 0.0 copy-start.7
  261.5 0.0 copy-start.8
  261.5 0.0 reduce-scatter.5.cloned.1.call-update
  261.5 0.3 all-reduce.3.cloned.1.call-start
  261.8 0.0 reduce-scatter.3.cloned.1.call-done
  261.8 0.0 copy-start.3
  261.8 39.1 %reduce-scatter.5.cloned.1.call-done = f32[128,512]{0,1:T(8,128)} async-done(((f32[512,512]{0,1:T(8,128)}), f32[128,512]{0,1:T(8,128)}) %reduce-scatter.5.cloned.1.call-update) | async-done | bytes 262160 | tf_op jit(solution)/shard_map/reduce_scatter | solution.py:45
  300.9 0.0 copy-done
  300.9 2.8 fusion.2
  303.7 0.0 copy-done.4
  303.7 2.0 fusion.4
  305.8 2.9 fusion.5
  308.7 0.0 copy-start.6
  308.7 3.0 fusion.3
  311.6 0.0 all-reduce.3.cloned.1.call-update
  311.7 0.0 copy-done.7
  311.7 0.0 copy-done.8
  311.7 0.2 fusion.12
  311.9 0.1 copy.28
  312.1 0.0 copy-start.5
  312.1 0.1 reshape.66
  312.1 1.0 convolution_bitcast_fusion
  313.2 2.1 copy.26
  315.2 0.0 copy-done.5
  315.2 9.1 %all-to-all-start.2 = ((f32[32,1,8192]{2,1,0:T(1,128)}), f32[32,1,8192]{2,1,0:T(1,128)S(1)}, u32[]{:S(2)}, u32[]{:S(2)}) async-start(f32[32,1,8192]{2,1,0:T(1,128)} %copy.26), calls=%async_computation.4 | async-start | bytes 2097152 | tf_op jit(solution)/shard_map/all_to_all | solution.py:82
  324.3 0.0 copy-done.3
  324.4 0.8 copy.27
  325.2 17.3 %all-to-all-done.2 = f32[32,1,8192]{2,1,0:T(1,128)S(1)} async-done(((f32[32,1,8192]{2,1,0:T(1,128)}), f32[32,1,8192]{2,1,0:T(1,128)S(1)}, u32[]{:S(2)}, u32[]{:S(2)}) %all-to-all-start.2) | async-done | bytes 1048608 | tf_op jit(solution)/shard_map/all_to_all | solution.py:82
  342.5 2.6 reduce.2
  345.0 0.2 reshape.67
  345.2 0.0 copy-done.6
  345.2 1.2 convolution_bitcast_fusion.4
  346.5 126.9 %all-reduce.3.cloned.1.call-done = (f32[512,512]{1,0:T(8,128)}, f32[512,512]{1,0:T(8,128)}, f32[512,512]{1,0:T(8,128)}) async-done(((f32[512,512]{1,0:T(8,128)}, f32[512,512]{1,0:T(8,128)}, f32[512,512]{1,0:T(8,128)}), (f32[512,512]{1,0:T(8,128)}, f32[512,512]{1,0:T(8,128)}, f32[512,512]{1,0:T(8,128)})) %all-reduce.3.cloned.1.call-update) | async-done | bytes 3145744 | tf_op jit(solution)/shard_map/psum | solution.py:64
  473.4 1.7 bitcast_subtract_fusion.1
  475.2 0.0 copy-start.1
  475.2 3.5 fusion.1
  478.7 0.0 copy-start.2
  478.7 4.8 fusion
  483.5 0.0 copy-done.1
  483.5 0.0 copy-done.2
  (3 shorter events, 0.0 us)
Async XLA Ops:
  7.2 293.7 %copy-start = (f32[512,512]{1,0:T(8,128)S(1)}, f32[512,512]{1,0:T(8,128)}, u32[]{:S(2)}) copy-start(f32[512,512]{1,0:T(8,128)} %param.12) | copy-start | bytes 3145732
  119.9 111.5 %all-to-all-start.1 = ((f32[32,128,512]{2,1,0:T(8,128)}), f32[32,128,512]{2,1,0:T(8,128)}, u32[]{:S(2)}, u32[]{:S(2)}) async-start(f32[32,128,512]{2,1,0:T(8,128)} %stack.7), calls=%async_computation.2 | async-start | bytes 16777216 | tf_op jit(solution)/shard_map/all_to_all | solution.py:13
  124.6 137.1 %reduce-scatter.3.cloned.1.call-start = ((), (), s32[]{:S(2)}) async-start(), calls=%async_computation.5 | async-start | bytes 1310720 | tf_op jit(solution)/shard_map/reduce_scatter | solution.py:45
  154.8 146.1 %reduce-scatter.5.cloned.1.call-start = ((), (), s32[]{:S(2)}) async-start(), calls=%async_computation.6 | async-start | bytes 1310720 | tf_op jit(solution)/shard_map/reduce_scatter | solution.py:45
  231.4 72.4 %copy-start.4 = (f32[2,128,512]{2,1,0:T(8,128)S(1)}, f32[2,128,512]{2,1,0:T(8,128)}, u32[]{:S(2)}) copy-start(f32[2,128,512]{2,1,0:T(8,128)} %param.9) | copy-start | bytes 1572868
  261.5 50.2 %copy-start.7 = (s32[1,1,32]{2,1,0:T(1,128)S(1)}, s32[1,1,32]{2,1,0:T(1,128)}, u32[]{:S(2)}) copy-start(s32[1,1,32]{2,1,0:T(1,128)} %param.13) | copy-start | bytes 388
  261.5 50.2 %copy-start.8 = (s32[1,1,32]{2,1,0:T(1,128)S(1)}, s32[1,1,32]{2,1,0:T(1,128)}, u32[]{:S(2)}) copy-start(s32[1,1,32]{2,1,0:T(1,128)} %param.14) | copy-start | bytes 388
  261.5 211.9 %all-reduce.3.cloned.1.call-start = ((), (), s32[]{:S(2)}) async-start(), calls=%async_computation.7 | async-start | bytes 6291456 | tf_op jit(solution)/shard_map/psum | solution.py:64
  261.8 62.5 %copy-start.3 = (f32[128,512]{0,1:T(8,128)S(1)}, f32[128,512]{0,1:T(8,128)}, u32[]{:S(2)}) copy-start(f32[128,512]{0,1:T(8,128)} %reduce-scatter.3.cloned.1.call-done) | copy-start | bytes 786436
  308.7 36.6 %copy-start.6 = (f32[1,1,512]{2,1,0:T(1,128)S(1)}, f32[1,1,512]{2,1,0:T(1,128)}, u32[]{:S(2)}) copy-start(f32[1,1,512]{2,1,0:T(1,128)} %param.15) | copy-start | bytes 6148
  312.1 3.2 copy-start.5
  315.2 27.2 %all-to-all-start.2 = ((f32[32,1,8192]{2,1,0:T(1,128)}), f32[32,1,8192]{2,1,0:T(1,128)S(1)}, u32[]{:S(2)}, u32[]{:S(2)}) async-start(f32[32,1,8192]{2,1,0:T(1,128)} %copy.26), calls=%async_computation.4 | async-start | bytes 2097152 | tf_op jit(solution)/shard_map/all_to_all | solution.py:82
  475.2 8.3 %copy-start.1 = (f32[512,512]{1,0:T(8,128)}, f32[512,512]{1,0:T(8,128)S(1)}, u32[]{:S(2)}) copy-start(f32[512,512]{1,0:T(8,128)S(1)} %bitcast_subtract_fusion.1) | copy-start | bytes 3145732
  478.7 4.8 copy-start.2
Sparse Core Ops, SparseCore 0:
  154.9 23.2 reduce-scatter.2
  261.6 39.2 reduce-scatter.4
  311.8 161.6 all-reduce.2
